TPU v7x, 256 devices: a whole 4x4x8 slice. The times are simulated.
256 devices in a mesh: seq: 32 (over y, x, core), tensor: 8 (over z).
Axes of the slice: x: 4, y: 4, z: 8, core: 2. Of those that a mesh axis runs over, the one named last changes fastest.
Arguments:
- queries: bfloat16 [4096, 8192], P('seq', 'tensor'), may hold values from -6 to 6
- key_vectors: bfloat16 [4096, 8192], P('seq', 'tensor'), may hold values from -6 to 6
- value_rows: bfloat16 [4096, 8192], P('seq', 'tensor'), may hold values from -6 to 6
- gate_logits: bfloat16 [4096, 8192], P('seq', 'tensor'), may hold values from -6 to 6
- log_decay: float32 [4096, 64], P('seq', 'tensor'), may hold values from -0.73 to 0, as said below
- initial_state: float32 [64, 128, 128], P('tensor'), may hold values from -192 to 192
- norm_gain: float32 [8192], P('tensor'), may hold values from 0.25 to 1.75
- out_weight: bfloat16 [8192, 6144], P('tensor', 'seq'), may hold values from -0.0625 to 0.0625
Outputs:
- mixed: float32 [4096, 6144], P('seq', 'tensor')
Inputs may be any that keep to these rules, and one draw needn't show every extreme that they name: `log_decay`: every entry is negative.
All inputs are finite; a program needn't handle non-finite values.
Results may differ from a plain program's by a relative error of at most 0.0075.
Values may be sent and summed in bfloat16 or wider, within the bound.
No kernel may reach another device: no remote copies, remote signals or barrier semaphores. Data moves between devices by JAX's collectives and lax.ppermute only.
A program may use at most 128 MiB of HBM per device.

v0:
```python
import jax
import jax.numpy as jnp
from jax import lax
from jax.sharding import Mesh, PartitionSpec as P

HIGH = lax.Precision.HIGHEST


def entering(array, axis, combine, identity):
    length, mine = (lax.axis_size(axis), lax.axis_index(axis))
    everything = jax.tree.map(lambda part: lax.all_gather(part, axis), array)
    start = jax.tree.map(
        lambda part, zero: jnp.broadcast_to(jnp.asarray(zero, part.dtype), part.shape),
        array,
        identity,
    )

    def hop(k, before):
        reached = k < mine
        new = combine(before, jax.tree.map(lambda part: part[k], everything))
        return jax.tree.map(lambda a, b: jnp.where(reached, a, b), new, before)

    return lax.fori_loop(0, length, hop, start)


def block_step(state, pieces):
    queries_b, keys_b, values_b, decay_b = pieces
    cumulative_memory = jnp.cumsum(decay_b, axis=0)
    total = cumulative_memory[-1]
    carried = jnp.exp(cumulative_memory)[:, :, None] * jnp.einsum(
        "thd,hde->the", queries_b.astype(jnp.float32), state, precision=HIGH
    )
    scores = jnp.einsum("thd,shd->hts", queries_b, keys_b, preferred_element_type=jnp.float32)
    length = cumulative_memory.shape[0]
    lower = jnp.tril(jnp.ones((length, length), dtype=bool))[None]
    spread = cumulative_memory.T[:, :, None] - cumulative_memory.T[:, None, :]
    weights = jnp.where(lower, jnp.exp(jnp.where(lower, spread, 0.0)), 0.0)
    mixes = (scores * weights).astype(jnp.bfloat16)
    local = jnp.einsum("hts,she->the", mixes, values_b, preferred_element_type=jnp.float32)
    scaled = keys_b.astype(jnp.float32) * jnp.exp(total[None, :] - cumulative_memory)[:, :, None]
    new_state = jnp.exp(total)[:, None, None] * state + jnp.einsum(
        "shd,she->hde", scaled, values_b.astype(jnp.float32), precision=HIGH
    )
    return (new_state, carried + local)


def normalize(attended, norm_gain, gate_logits):
    mean_square = jnp.mean(attended * attended, axis=-1, keepdims=True)
    normalized_output = attended * lax.rsqrt(mean_square + 1e-05)
    flat = normalized_output.reshape(attended.shape[0], -1)
    gated = flat * norm_gain[None, :] * jax.nn.sigmoid(gate_logits.astype(jnp.float32))
    return gated.astype(jnp.bfloat16)


def chain_link(earlier, later):
    return (earlier[0] * later[0], later[0][:, None, None] * earlier[1] + later[1])


def pack(rates, state):
    heads = state.shape[0]
    flat = state.reshape(heads, -1)
    lanes = jnp.broadcast_to(rates[:, None], (heads, 128))
    return jnp.concatenate([flat, lanes], axis=1)


def link_packed(earlier, later):
    width = later.shape[1] - 128
    later_rate = later[:, width : width + 1]
    state = later_rate * earlier[:, :width] + later[:, :width]
    rate = earlier[:, width:] * later[:, width:]
    return jnp.concatenate([state, rate], axis=1)


def swap_cores(array):
    return lax.ppermute(array, "core", [(0, 1), (1, 0)])


def carried_in(rates, state, initial_state):
    chips, chip = (lax.axis_size("chip"), lax.axis_index("chip"))
    core = lax.axis_index("core")
    half = state.shape[0] // 2
    own = pack(rates, state)
    own_mine = lax.dynamic_slice_in_dim(own, core * half, half, axis=0)
    own_other = lax.dynamic_slice_in_dim(own, (1 - core) * half, half, axis=0)
    partner_mine = swap_cores(own_other)
    first_core = jnp.where(core == 0, own_mine, partner_mine)
    second_core = jnp.where(core == 0, partner_mine, own_mine)
    chip_element = link_packed(first_core, second_core)
    shifted = lax.ppermute(chip_element, "chip", [(i, i + 1) for i in range(chips - 1)])
    start_state = lax.dynamic_slice_in_dim(initial_state, core * half, half, axis=0)
    first = pack(jnp.ones((half,), rates.dtype), start_state)
    current = jnp.where(chip == 0, first, shifted)
    step = 1
    while step < chips:
        earlier = lax.ppermute(current, "chip", [(i, i + step) for i in range(chips - step)])
        current = jnp.where(chip >= step, link_packed(earlier, current), current)
        step *= 2
    for_second = link_packed(current, first_core)
    keep = jnp.where(core == 0, current, for_second)
    other = swap_cores(jnp.where(core == 0, for_second, current))
    whole = jnp.where(core == 0, jnp.concatenate([keep, other]), jnp.concatenate([other, keep]))
    width = whole.shape[1] - 128
    return whole[:, :width].reshape(state.shape)


def per_device(
    queries, key_vectors, value_rows, gate_logits, log_decay, initial_state, norm_gain, out_weight
):
    rows_here = queries.shape[0]
    head_count = log_decay.shape[1]
    head_dim = initial_state.shape[1]
    block_len = min(512, rows_here)
    block_count = rows_here // block_len

    def shaped(array):
        return array.reshape(block_count, block_len, head_count, head_dim)

    zero_state = jnp.zeros((head_count, head_dim, head_dim), jnp.float32)
    decay_blocks = log_decay.reshape(block_count, block_len, head_count)
    device_state, outputs = lax.scan(
        block_step,
        zero_state,
        (shaped(queries), shaped(key_vectors), shaped(value_rows), decay_blocks),
    )
    local_out = outputs.reshape(rows_here, head_count, head_dim)
    through = jnp.cumsum(log_decay, axis=0)
    shard_fading_rates = jnp.exp(through[-1])
    incoming = carried_in(shard_fading_rates, device_state, initial_state)
    query_float = queries.reshape(rows_here, head_count, head_dim).astype(jnp.float32)
    inherited = jnp.exp(through)[:, :, None] * jnp.einsum(
        "thd,hde->the", query_float, incoming, precision=HIGH
    )
    attended = local_out + inherited
    hidden = normalize(attended, norm_gain, gate_logits)
    terms = jnp.dot(
        hidden,
        lax.all_gather(out_weight, ("chip", "core"), axis=1, tiled=True),
        preferred_element_type=jnp.float32,
    )
    mixed = lax.psum_scatter(terms, "tensor", scatter_dimension=1, tiled=True)
    return mixed


def solution(mesh):
    seq_len, groups = mesh.devices.shape
    split = Mesh(mesh.devices.reshape(seq_len // 2, 2, groups), ("chip", "core", "tensor"))
    tokens = ("chip", "core")
    return jax.shard_map(
        per_device,
        mesh=split,
        in_specs=(
            P(tokens, "tensor"),
            P(tokens, "tensor"),
            P(tokens, "tensor"),
            P(tokens, "tensor"),
            P(tokens, "tensor"),
            P("tensor", None, None),
            P("tensor"),
            P("tensor", tokens),
        ),
        out_specs=P(tokens, "tensor"),
        check_vma=False,
    )
```

profile of v0, /device:TPU:14, one launch (start us, length us, event | category | flops | bytes accessed | tf_op | source)
XLA Modules:
  0.0 184.1 jit_solution(1943625744013885073)
XLA Ops:
  6.5 0.0 copy-start
  6.5 0.0 copy-start.2
  6.5 0.0 copy-start.1
  6.5 0.0 copy-start.4
  6.5 0.0 all-gather.2.cloned.1.call-start
  6.6 0.9 copy.35
  7.5 0.2 reduce_window_sum.13
  7.8 1.1 copy.52
  8.9 1.4 fusion.4
  10.3 0.3 copy.89
  10.6 0.1 broadcast_in_dim.56
  10.6 0.1 fusion.17
  10.7 0.1 collective-permute-start
  10.8 1.5 collective-permute-done
  12.3 0.1 broadcast_select_fusion
  12.4 0.1 slice_reduce_fusion.5
  12.6 0.2 slice_add_fusion.4
  12.7 0.1 pad_maximum_fusion.2
  12.8 3.4 %collective-permute-start.1 = (f32[4,16512]{1,0:T(4,128)S(1)}, f32[4,16512]{1,0:T(4,128)S(1)}, u32[]{:S(2)}, u32[]{:S(2)}) collective-permute-start(f32[4,16512]{1,0:T(4,128)S(1)} %pad_maximum_fusion.2), channel_id=1, source_target_pairs={{0,16},{16,32},{32,48},{48,64},{64,80},{80,96},{96,112},{112,128},... | collective-permute-start | bytes 792584 | tf_op jit(solution)/shard_map/ppermute | solution.py:89
  16.2 0.0 copy-done
  16.2 0.2 copy.90
  16.4 6.6 %collective-permute-done.1 = f32[4,16512]{1,0:T(4,128)S(1)} collective-permute-done((f32[4,16512]{1,0:T(4,128)S(1)}, f32[4,16512]{1,0:T(4,128)S(1)}, u32[]{:S(2)}, u32[]{:S(2)}) %collective-permute-start.1) | collective-permute-done | bytes 264224 | tf_op jit(solution)/shard_map/ppermute | solution.py:89
  23.1 0.1 pad_select_fusion
  23.1 5.5 %collective-permute-start.2 = (f32[4,16512]{1,0:T(4,128)S(1)}, f32[4,16512]{1,0:T(4,128)S(1)}, u32[]{:S(2)}, u32[]{:S(2)}) collective-permute-start(f32[4,16512]{1,0:T(4,128)S(1)} %pad_select_fusion), channel_id=1, source_target_pairs={{0,16},{16,32},{32,48},{48,64},{64,80},{80,96},{96,112},{112,128},... | collective-permute-start | bytes 792584 | tf_op jit(solution)/shard_map/ppermute | solution.py:95
  28.7 0.1 slice_reduce_fusion.4
  28.8 4.9 %collective-permute-done.2 = f32[4,16512]{1,0:T(4,128)S(1)} collective-permute-done((f32[4,16512]{1,0:T(4,128)S(1)}, f32[4,16512]{1,0:T(4,128)S(1)}, u32[]{:S(2)}, u32[]{:S(2)}) %collective-permute-start.2) | collective-permute-done | bytes 264224 | tf_op jit(solution)/shard_map/ppermute | solution.py:95
  33.7 0.1 slice_add_fusion.3
  33.8 0.1 maximum_select_fusion
  33.9 4.1 %collective-permute-start.3 = (f32[4,16512]{1,0:T(4,128)S(1)}, f32[4,16512]{1,0:T(4,128)S(1)}, u32[]{:S(2)}, u32[]{:S(2)}) collective-permute-start(f32[4,16512]{1,0:T(4,128)S(1)} %maximum_select_fusion), channel_id=1, source_target_pairs={{0,32},{16,48},{32,64},{48,80},{64,96},{80,112},{96,128},{112,144}... | collective-permute-start | bytes 792584 | tf_op jit(solution)/shard_map/ppermute | solution.py:95
  38.1 0.1 slice_reduce_fusion.3
  38.2 5.8 %collective-permute-done.3 = f32[4,16512]{1,0:T(4,128)S(1)} collective-permute-done((f32[4,16512]{1,0:T(4,128)S(1)}, f32[4,16512]{1,0:T(4,128)S(1)}, u32[]{:S(2)}, u32[]{:S(2)}) %collective-permute-start.3) | collective-permute-done | bytes 264224 | tf_op jit(solution)/shard_map/ppermute | solution.py:95
  44.0 0.1 slice_add_fusion.2
  44.2 0.1 maximum_select_fusion.1
  44.3 3.2 %collective-permute-start.4 = (f32[4,16512]{1,0:T(4,128)S(1)}, f32[4,16512]{1,0:T(4,128)S(1)}, u32[]{:S(2)}, u32[]{:S(2)}) collective-permute-start(f32[4,16512]{1,0:T(4,128)S(1)} %maximum_select_fusion.1), channel_id=1, source_target_pairs={{0,64},{16,80},{32,96},{48,112},{64,128},{80,144},{96,160},{112,17... | collective-permute-start | bytes 792584 | tf_op jit(solution)/shard_map/ppermute | solution.py:95
  47.5 0.0 all-gather.2.cloned.1.call-update
  47.5 0.0 reduce-scatter.2.cloned.1.call-start
  47.5 0.1 slice_reduce_fusion.2
  47.6 4.9 %collective-permute-done.4 = f32[4,16512]{1,0:T(4,128)S(1)} collective-permute-done((f32[4,16512]{1,0:T(4,128)S(1)}, f32[4,16512]{1,0:T(4,128)S(1)}, u32[]{:S(2)}, u32[]{:S(2)}) %collective-permute-start.4) | collective-permute-done | bytes 264224 | tf_op jit(solution)/shard_map/ppermute | solution.py:95
  52.5 0.1 slice_add_fusion.1
  52.7 0.1 maximum_select_fusion.2
  52.8 3.1 %collective-permute-start.5 = (f32[4,16512]{1,0:T(4,128)S(1)}, f32[4,16512]{1,0:T(4,128)S(1)}, u32[]{:S(2)}, u32[]{:S(2)}) collective-permute-start(f32[4,16512]{1,0:T(4,128)S(1)} %maximum_select_fusion.2), channel_id=1, source_target_pairs={{0,128},{16,144},{32,160},{48,176},{64,192},{80,208},{96,224},{112... | collective-permute-start | bytes 792584 | tf_op jit(solution)/shard_map/ppermute | solution.py:95
  55.9 0.1 slice_reduce_fusion
  56.0 0.1 slice_reduce_fusion.1
  56.1 3.6 %collective-permute-done.5 = f32[4,16512]{1,0:T(4,128)S(1)} collective-permute-done((f32[4,16512]{1,0:T(4,128)S(1)}, f32[4,16512]{1,0:T(4,128)S(1)}, u32[]{:S(2)}, u32[]{:S(2)}) %collective-permute-start.5) | collective-permute-done | bytes 264224 | tf_op jit(solution)/shard_map/ppermute | solution.py:95
  59.8 0.1 slice_add_fusion
  59.9 0.1 maximum_select_fusion.3
  60.0 0.1 fusion.25
  60.2 0.1 fusion.41
  60.3 0.1 collective-permute-start.6
  60.4 0.1 copy.36
  60.5 0.0 copy-done.1
  60.5 0.7 fusion.2
  61.2 0.7 collective-permute-done.6
  61.9 0.2 fusion.9
  62.1 0.6 fusion.3
  62.7 0.0 copy-done.2
  62.7 0.5 multiply_reduce_fusion
  63.3 0.2 copy.49
  63.5 54.9 %all-gather.2.cloned.1.call-done = bf16[1024,6144]{0,1:T(8,128)(2,1)} async-done(((bf16[1024,192]{0,1:T(8,128)(2,1)}), bf16[1024,6144]{0,1:T(8,128)(2,1)}) %all-gather.2.cloned.1.call-update) | async-done | bytes 12582928 | tf_op jit(solution)/shard_map/all_gather | solution.py:137
  118.4 0.0 copy-done.4
  118.4 0.0 copy-done.3
  118.4 10.5 %fusion.18 = f32[128,6144]{1,0:T(8,128)} fusion(bf16[1024,6144]{0,1:T(8,128)(2,1)} %all-gather.2.cloned.1.call-done, bf16[128,1024]{1,0:T(8,128)(2,1)S(1)} %copy-done.3, f32[128,1024]{1,0:T(8,128)S(1)} %copy.49, f32[1024]{0:T(1024)S(1)} %copy-done.4), kind=kOutput, calls=%fused_computation.39 | convolution fusion | flops 1611530240 | bytes 16519168 | tf_op jit(solution)/shard_map/dot_general | solution.py:135
  128.9 0.0 reduce-scatter.2.cloned.1.call-update
  128.9 48.3 %reduce-scatter.2.cloned.1.call-done = f32[128,768]{1,0:T(8,128)} async-done(((f32[128,6144]{1,0:T(8,128)}), f32[128,768]{1,0:T(8,128)}) %reduce-scatter.2.cloned.1.call-update) | async-done | bytes 393232 | tf_op jit(solution)/shard_map/reduce_scatter | solution.py:140
  (16 shorter events, 0.3 us)
Async XLA Ops:
  6.5 9.7 %copy-start = (f32[8,128,128]{2,1,0:T(8,128)S(1)}, f32[8,128,128]{2,1,0:T(8,128)}, u32[]{:S(2)}) copy-start(f32[8,128,128]{2,1,0:T(8,128)} %param.13) | copy-start | bytes 1572868
  6.5 56.2 %copy-start.2 = (bf16[128,1024]{1,0:T(8,128)(2,1)S(1)}, bf16[128,1024]{1,0:T(8,128)(2,1)}, u32[]{:S(2)}) copy-start(bf16[128,1024]{1,0:T(8,128)(2,1)} %param.10) | copy-start | bytes 786436
  6.5 54.0 %copy-start.1 = (bf16[128,1024]{1,0:T(8,128)(2,1)S(1)}, bf16[128,1024]{1,0:T(8,128)(2,1)}, u32[]{:S(2)}) copy-start(bf16[128,1024]{1,0:T(8,128)(2,1)} %param.8) | copy-start | bytes 786436
  6.5 111.9 %copy-start.4 = (f32[1024]{0:T(1024)S(1)}, f32[1024]{0:T(1024)}, u32[]{:S(2)}) copy-start(f32[1024]{0:T(1024)} %param.14) | copy-start | bytes 12292
  6.5 111.9 %copy-start.3 = (bf16[128,1024]{1,0:T(8,128)(2,1)S(1)}, bf16[128,1024]{1,0:T(8,128)(2,1)}, u32[]{:S(2)}) copy-start(bf16[128,1024]{1,0:T(8,128)(2,1)} %param.11) | copy-start | bytes 786436
  6.5 111.9 %all-gather.2.cloned.1.call-start = ((), (), s32[]{:S(2)}) async-start(), calls=%async_computation.1 | async-start | bytes 12976128 | tf_op jit(solution)/shard_map/all_gather | solution.py:137
  10.7 1.6 collective-permute-start
  12.8 10.3 %collective-permute-start.1 = (f32[4,16512]{1,0:T(4,128)S(1)}, f32[4,16512]{1,0:T(4,128)S(1)}, u32[]{:S(2)}, u32[]{:S(2)}) collective-permute-start(f32[4,16512]{1,0:T(4,128)S(1)} %pad_maximum_fusion.2), channel_id=1, source_target_pairs={{0,16},{16,32},{32,48},{48,64},{64,80},{80,96},{96,112},{112,128},... | collective-permute-start | bytes 792584 | tf_op jit(solution)/shard_map/ppermute | solution.py:89
  23.1 10.5 %collective-permute-start.2 = (f32[4,16512]{1,0:T(4,128)S(1)}, f32[4,16512]{1,0:T(4,128)S(1)}, u32[]{:S(2)}, u32[]{:S(2)}) collective-permute-start(f32[4,16512]{1,0:T(4,128)S(1)} %pad_select_fusion), channel_id=1, source_target_pairs={{0,16},{16,32},{32,48},{48,64},{64,80},{80,96},{96,112},{112,128},... | collective-permute-start | bytes 792584 | tf_op jit(solution)/shard_map/ppermute | solution.py:95
  33.9 10.1 %collective-permute-start.3 = (f32[4,16512]{1,0:T(4,128)S(1)}, f32[4,16512]{1,0:T(4,128)S(1)}, u32[]{:S(2)}, u32[]{:S(2)}) collective-permute-start(f32[4,16512]{1,0:T(4,128)S(1)} %maximum_select_fusion), channel_id=1, source_target_pairs={{0,32},{16,48},{32,64},{48,80},{64,96},{80,112},{96,128},{112,144}... | collective-permute-start | bytes 792584 | tf_op jit(solution)/shard_map/ppermute | solution.py:95
  44.3 8.3 %collective-permute-start.4 = (f32[4,16512]{1,0:T(4,128)S(1)}, f32[4,16512]{1,0:T(4,128)S(1)}, u32[]{:S(2)}, u32[]{:S(2)}) collective-permute-start(f32[4,16512]{1,0:T(4,128)S(1)} %maximum_select_fusion.1), channel_id=1, source_target_pairs={{0,64},{16,80},{32,96},{48,112},{64,128},{80,144},{96,160},{112,17... | collective-permute-start | bytes 792584 | tf_op jit(solution)/shard_map/ppermute | solution.py:95
  47.5 129.8 %reduce-scatter.2.cloned.1.call-start = ((), (), s32[]{:S(2)}) async-start(), calls=%async_computation.2 | async-start | bytes 3538944 | tf_op jit(solution)/shard_map/reduce_scatter | solution.py:140
  52.8 7.0 %collective-permute-start.5 = (f32[4,16512]{1,0:T(4,128)S(1)}, f32[4,16512]{1,0:T(4,128)S(1)}, u32[]{:S(2)}, u32[]{:S(2)}) collective-permute-start(f32[4,16512]{1,0:T(4,128)S(1)} %maximum_select_fusion.2), channel_id=1, source_target_pairs={{0,128},{16,144},{32,160},{48,176},{64,192},{80,208},{96,224},{112... | collective-permute-start | bytes 792584 | tf_op jit(solution)/shard_map/ppermute | solution.py:95
  60.3 1.6 collective-permute-start.6
Sparse Core Ops, SparseCore 0:
  47.6 70.7 all-gather.1
  129.0 48.1 reduce-scatter.1
where the time goes:
time: 184 us
  waiting for transfers between devices  131 us (71%)
  starting transfers between devices  19.6 us (11%)
  between operations  13.7 us (7%)
  matrix products  13.6 us (7%)
  local copies, waits for them, and re-layouts  3.67 us (2%)
  other arithmetic  2.07 us (1%)
    all_gather x1, waiting for transfers between devices, per_device(): lax.all_gather(out_weight, ('chip', 'core'), axis=1, tiled=True)  54.9 us
    reduce_scatter x1, waiting for transfers between devices, per_device(): mixed = lax.psum_scatter(terms, 'tensor', scatter_dimension=1, tiled=True)  48.3 us
    ppermute x4, waiting for transfers between devices, carried_in(): lax.ppermute(current, 'chip', [(i, i + step) for i in range(chips - step)])  19.3 us
    ppermute x4, starting transfers between devices, carried_in(): lax.ppermute(current, 'chip', [(i, i + step) for i in range(chips - step)])  15.9 us
    dot_general x1, matrix products, per_device(): jnp.dot(hidden, lax.all_gather(out_weight, ('chip', 'core'), axis=1, tile...  10.5 us
    ppermute x1, waiting for transfers between devices, carried_in(): lax.ppermute(chip_element, 'chip', [(i, i + 1) for i in range(chips - 1)])  6.65 us
  transfers between devices with their start and end apart: 9, of which 9 were waited for; matrix products, arithmetic and copies ran while one was open for 2% of the time, Pallas kernels for 0%

commit v1 on v0

--- a/solution.py
+++ b/solution.py
@@ -134,7 +134,12 @@
     hidden = normalize(attended, norm_gain, gate_logits)
     terms = jnp.dot(
         hidden,
-        lax.all_gather(out_weight, ("chip", "core"), axis=1, tiled=True),
+        jnp.concatenate(
+            lax.all_to_all(
+                jnp.stack([out_weight] * lax.axis_size(("chip", "core"))), ("chip", "core"), 0, 0
+            ),
+            axis=1,
+        ),
         preferred_element_type=jnp.float32,
     )
     mixed = lax.psum_scatter(terms, "tensor", scatter_dimension=1, tiled=True)

time: 184 us -> 297 us (1.61)
  waiting for transfers between devices: 131 us -> 226 us
  starting transfers between devices: 19.6 us -> 30.9 us
  local copies, waits for them, and re-layouts: 3.67 us -> 9.73 us
    all_to_all x0 -> x1, waiting for transfers between devices: none -> 141 us  [per_device(): lax.all_to_all(jnp.stack([out_weight] * lax.axis_size(('chip', 'core'))),...]
    all_gather x1 -> x0, waiting for transfers between devices: 54.9 us -> none  [per_device(): lax.all_gather(out_weight, ('chip', 'core'), axis=1, tiled=True)]
    reduce_scatter x1, waiting for transfers between devices: 48.3 us -> 60.8 us  [per_device(): mixed = lax.psum_scatter(terms, 'tensor', scatter_dimension=1, tiled=True)]
    all_to_all x0 -> x1, starting transfers between devices: none -> 11.2 us  [per_device(): lax.all_to_all(jnp.stack([out_weight] * lax.axis_size(('chip', 'core'))),...]
    another operation x0 -> x1, local copies, waits for them, and re-layouts: none -> 6.09 us  [per_device(): jnp.stack([out_weight] * lax.axis_size(('chip', 'core')))]
    ppermute x4, waiting for transfers between devices: 19.3 us -> 15.7 us  [carried_in(): lax.ppermute(current, 'chip', [(i, i + step) for i in range(chips - step)])]
  transfers between devices with their start and end apart: 9 -> 9, of which waited for: 9 -> 8; matrix products, arithmetic and copies ran while one was open for 2% -> 3% of each run, Pallas kernels for 0% -> 0%
where the time goes in v1:
time: 297 us; the launch traced here: 296 us
  waiting for transfers between devices  226 us (76%)
  starting transfers between devices  30.9 us (10%)
  between operations  13.7 us (5%)
  matrix products  13.6 us (5%)
  local copies, waits for them, and re-layouts  9.73 us (3%)
    all_to_all x1, waiting for transfers between devices, per_device(): lax.all_to_all(jnp.stack([out_weight] * lax.axis_size(('chip', 'core'))),...  141 us
    reduce_scatter x1, waiting for transfers between devices, per_device(): mixed = lax.psum_scatter(terms, 'tensor', scatter_dimension=1, tiled=True)  60.8 us
    ppermute x4, starting transfers between devices, carried_in(): lax.ppermute(current, 'chip', [(i, i + step) for i in range(chips - step)])  15.9 us
    ppermute x4, waiting for transfers between devices, carried_in(): lax.ppermute(current, 'chip', [(i, i + step) for i in range(chips - step)])  15.7 us
    all_to_all x1, starting transfers between devices, per_device(): lax.all_to_all(jnp.stack([out_weight] * lax.axis_size(('chip', 'core'))),...  11.2 us
    dot_general x1, matrix products, per_device(): jnp.dot(hidden, jnp.concatenate(lax.all_to_all(jnp.stack([out_weight] * l...  10.4 us
    ppermute x1, waiting for transfers between devices, carried_in(): lax.ppermute(chip_element, 'chip', [(i, i + 1) for i in range(chips - 1)])  6.65 us
    another operation x1, local copies, waits for them, and re-layouts, per_device(): jnp.stack([out_weight] * lax.axis_size(('chip', 'core')))  6.09 us
  transfers between devices with their start and end apart: 9, of which 8 were waited for; matrix products, arithmetic and copies ran while one was open for 3% of the time, Pallas kernels for 0%

profile of v1, /device:TPU:14, one launch (start us, length us, event | category | flops | bytes accessed | tf_op | source)
XLA Modules:
  0.0 296.1 jit_solution(13179666561960264411)
XLA Ops:
  6.5 0.0 copy-start
  6.5 0.0 copy-start.3
  6.5 0.9 copy.36
  7.4 0.2 reduce_window_sum.13
  7.6 1.1 copy.53
  8.8 1.4 fusion.4
  10.2 0.3 copy.90
  10.5 0.1 broadcast_in_dim.56
  10.6 0.1 fusion.17
  10.6 0.1 collective-permute-start
  10.7 1.5 collective-permute-done
  12.3 0.1 broadcast_select_fusion
  12.4 0.1 slice_reduce_fusion.5
  12.5 0.2 slice_add_fusion.4
  12.6 0.1 pad_maximum_fusion.2
  12.7 3.4 %collective-permute-start.1 = (f32[4,16512]{1,0:T(4,128)S(1)}, f32[4,16512]{1,0:T(4,128)S(1)}, u32[]{:S(2)}, u32[]{:S(2)}) collective-permute-start(f32[4,16512]{1,0:T(4,128)S(1)} %pad_maximum_fusion.2), channel_id=1, source_target_pairs={{0,16},{16,32},{32,48},{48,64},{64,80},{80,96},{96,112},{112,128},... | collective-permute-start | bytes 792584 | tf_op jit(solution)/shard_map/ppermute | solution.py:89
  16.1 0.0 copy-done
  16.2 0.2 copy.91
  16.3 6.6 %collective-permute-done.1 = f32[4,16512]{1,0:T(4,128)S(1)} collective-permute-done((f32[4,16512]{1,0:T(4,128)S(1)}, f32[4,16512]{1,0:T(4,128)S(1)}, u32[]{:S(2)}, u32[]{:S(2)}) %collective-permute-start.1) | collective-permute-done | bytes 264224 | tf_op jit(solution)/shard_map/ppermute | solution.py:89
  23.0 0.1 pad_select_fusion
  23.1 5.5 %collective-permute-start.2 = (f32[4,16512]{1,0:T(4,128)S(1)}, f32[4,16512]{1,0:T(4,128)S(1)}, u32[]{:S(2)}, u32[]{:S(2)}) collective-permute-start(f32[4,16512]{1,0:T(4,128)S(1)} %pad_select_fusion), channel_id=1, source_target_pairs={{0,16},{16,32},{32,48},{48,64},{64,80},{80,96},{96,112},{112,128},... | collective-permute-start | bytes 792584 | tf_op jit(solution)/shard_map/ppermute | solution.py:95
  28.6 0.1 slice_reduce_fusion.4
  28.7 4.9 %collective-permute-done.2 = f32[4,16512]{1,0:T(4,128)S(1)} collective-permute-done((f32[4,16512]{1,0:T(4,128)S(1)}, f32[4,16512]{1,0:T(4,128)S(1)}, u32[]{:S(2)}, u32[]{:S(2)}) %collective-permute-start.2) | collective-permute-done | bytes 264224 | tf_op jit(solution)/shard_map/ppermute | solution.py:95
  33.6 0.1 slice_add_fusion.3
  33.8 0.1 maximum_select_fusion
  33.9 4.1 %collective-permute-start.3 = (f32[4,16512]{1,0:T(4,128)S(1)}, f32[4,16512]{1,0:T(4,128)S(1)}, u32[]{:S(2)}, u32[]{:S(2)}) collective-permute-start(f32[4,16512]{1,0:T(4,128)S(1)} %maximum_select_fusion), channel_id=1, source_target_pairs={{0,32},{16,48},{32,64},{48,80},{64,96},{80,112},{96,128},{112,144}... | collective-permute-start | bytes 792584 | tf_op jit(solution)/shard_map/ppermute | solution.py:95
  38.0 0.1 slice_reduce_fusion.3
  38.1 5.8 %collective-permute-done.3 = f32[4,16512]{1,0:T(4,128)S(1)} collective-permute-done((f32[4,16512]{1,0:T(4,128)S(1)}, f32[4,16512]{1,0:T(4,128)S(1)}, u32[]{:S(2)}, u32[]{:S(2)}) %collective-permute-start.3) | collective-permute-done | bytes 264224 | tf_op jit(solution)/shard_map/ppermute | solution.py:95
  44.0 0.1 slice_add_fusion.2
  44.1 0.1 maximum_select_fusion.1
  44.2 3.2 %collective-permute-start.4 = (f32[4,16512]{1,0:T(4,128)S(1)}, f32[4,16512]{1,0:T(4,128)S(1)}, u32[]{:S(2)}, u32[]{:S(2)}) collective-permute-start(f32[4,16512]{1,0:T(4,128)S(1)} %maximum_select_fusion.1), channel_id=1, source_target_pairs={{0,64},{16,80},{32,96},{48,112},{64,128},{80,144},{96,160},{112,17... | collective-permute-start | bytes 792584 | tf_op jit(solution)/shard_map/ppermute | solution.py:95
  47.4 0.1 slice_reduce_fusion.2
  47.5 5.0 %collective-permute-done.4 = f32[4,16512]{1,0:T(4,128)S(1)} collective-permute-done((f32[4,16512]{1,0:T(4,128)S(1)}, f32[4,16512]{1,0:T(4,128)S(1)}, u32[]{:S(2)}, u32[]{:S(2)}) %collective-permute-start.4) | collective-permute-done | bytes 264224 | tf_op jit(solution)/shard_map/ppermute | solution.py:95
  52.5 0.1 slice_add_fusion.1
  52.6 0.1 maximum_select_fusion.2
  52.7 3.1 %collective-permute-start.5 = (f32[4,16512]{1,0:T(4,128)S(1)}, f32[4,16512]{1,0:T(4,128)S(1)}, u32[]{:S(2)}, u32[]{:S(2)}) collective-permute-start(f32[4,16512]{1,0:T(4,128)S(1)} %maximum_select_fusion.2), channel_id=1, source_target_pairs={{0,128},{16,144},{32,160},{48,176},{64,192},{80,208},{96,224},{112... | collective-permute-start | bytes 792584 | tf_op jit(solution)/shard_map/ppermute | solution.py:95
  55.8 0.0 copy-done.3
  55.8 6.1 %stack.2 = bf16[32,1024,192]{1,2,0:T(8,128)(2,1)} broadcast(bf16[1024,192]{0,1:T(8,128)(2,1)S(1)} %copy-done.3), dimensions={1,2} | broadcast | bytes 12976128 | tf_op jit(solution)/shard_map/stack | solution.py:139
  61.9 0.0 copy-start.1
  61.9 11.2 %all-to-all-start = ((bf16[32,1024,192]{1,2,0:T(8,128)(2,1)}), bf16[32,1024,192]{1,2,0:T(8,128)(2,1)}, u32[]{:S(2)}, u32[]{:S(2)}) async-start(bf16[32,1024,192]{1,2,0:T(8,128)(2,1)} %stack.2), calls=%async_computation | async-start | bytes 25165824 | tf_op jit(solution)/shard_map/all_to_all | solution.py:138
  73.2 0.0 reduce-scatter.2.cloned.1.call-start
  73.2 0.1 slice_reduce_fusion
  73.4 0.1 slice_reduce_fusion.1
  73.5 0.0 collective-permute-done.5
  73.5 0.1 slice_add_fusion
  73.6 0.1 maximum_select_fusion.3
  73.7 0.1 fusion.25
  73.9 0.1 fusion.41
  74.0 0.2 collective-permute-start.6
  74.3 0.1 copy.42
  74.3 0.0 copy-done.1
  74.3 0.7 fusion.2
  75.0 0.6 collective-permute-done.6
  75.6 0.2 fusion.9
  75.8 0.6 fusion.3
  76.4 0.0 copy-done.2
  76.4 0.5 multiply_reduce_fusion
  77.0 0.2 copy.50
  77.2 140.7 %all-to-all-done = bf16[32,1024,192]{1,2,0:T(8,128)(2,1)} async-done(((bf16[32,1024,192]{1,2,0:T(8,128)(2,1)}), bf16[32,1024,192]{1,2,0:T(8,128)(2,1)}, u32[]{:S(2)}, u32[]{:S(2)}) %all-to-all-start) | async-done | bytes 12582944 | tf_op jit(solution)/shard_map/all_to_all | solution.py:138
  217.9 0.0 copy-done.4
  217.9 0.0 copy-done.5
  217.9 10.4 %fusion.18 = f32[128,6144]{1,0:T(8,128)} fusion(bf16[1024,6144]{0,1:T(8,128)(2,1)} %bitcast.7, bf16[128,1024]{1,0:T(8,128)(2,1)S(1)} %copy-done.4, f32[128,1024]{1,0:T(8,128)S(1)} %copy.50, f32[1024]{0:T(1024)S(1)} %copy-done.5), kind=kOutput, calls=%fused_computation.39 | convolution fusion | flops 1611530240 | bytes 16519168 | tf_op jit(solution)/shard_map/dot_general | solution.py:135
  228.4 0.0 reduce-scatter.2.cloned.1.call-update
  228.4 60.8 %reduce-scatter.2.cloned.1.call-done = f32[128,768]{1,0:T(8,128)} async-done(((f32[128,6144]{1,0:T(8,128)}), f32[128,768]{1,0:T(8,128)}) %reduce-scatter.2.cloned.1.call-update) | async-done | bytes 393232 | tf_op jit(solution)/shard_map/reduce_scatter | solution.py:145
  (18 shorter events, 0.3 us)
Async XLA Ops:
  6.5 9.6 %copy-start = (f32[8,128,128]{2,1,0:T(8,128)S(1)}, f32[8,128,128]{2,1,0:T(8,128)}, u32[]{:S(2)}) copy-start(f32[8,128,128]{2,1,0:T(8,128)} %param.13) | copy-start | bytes 1572868
  6.5 49.3 %copy-start.3 = (bf16[1024,192]{0,1:T(8,128)(2,1)S(1)}, bf16[1024,192]{0,1:T(8,128)(2,1)}, u32[]{:S(2)}) copy-start(bf16[1024,192]{0,1:T(8,128)(2,1)} %param.15) | copy-start | bytes 1179652
  10.6 1.6 collective-permute-start
  12.7 10.3 %collective-permute-start.1 = (f32[4,16512]{1,0:T(4,128)S(1)}, f32[4,16512]{1,0:T(4,128)S(1)}, u32[]{:S(2)}, u32[]{:S(2)}) collective-permute-start(f32[4,16512]{1,0:T(4,128)S(1)} %pad_maximum_fusion.2), channel_id=1, source_target_pairs={{0,16},{16,32},{32,48},{48,64},{64,80},{80,96},{96,112},{112,128},... | collective-permute-start | bytes 792584 | tf_op jit(solution)/shard_map/ppermute | solution.py:89
  23.1 10.5 %collective-permute-start.2 = (f32[4,16512]{1,0:T(4,128)S(1)}, f32[4,16512]{1,0:T(4,128)S(1)}, u32[]{:S(2)}, u32[]{:S(2)}) collective-permute-start(f32[4,16512]{1,0:T(4,128)S(1)} %pad_select_fusion), channel_id=1, source_target_pairs={{0,16},{16,32},{32,48},{48,64},{64,80},{80,96},{96,112},{112,128},... | collective-permute-start | bytes 792584 | tf_op jit(solution)/shard_map/ppermute | solution.py:95
  33.9 10.1 %collective-permute-start.3 = (f32[4,16512]{1,0:T(4,128)S(1)}, f32[4,16512]{1,0:T(4,128)S(1)}, u32[]{:S(2)}, u32[]{:S(2)}) collective-permute-start(f32[4,16512]{1,0:T(4,128)S(1)} %maximum_select_fusion), channel_id=1, source_target_pairs={{0,32},{16,48},{32,64},{48,80},{64,96},{80,112},{96,128},{112,144}... | collective-permute-start | bytes 792584 | tf_op jit(solution)/shard_map/ppermute | solution.py:95
  44.2 8.3 %collective-permute-start.4 = (f32[4,16512]{1,0:T(4,128)S(1)}, f32[4,16512]{1,0:T(4,128)S(1)}, u32[]{:S(2)}, u32[]{:S(2)}) collective-permute-start(f32[4,16512]{1,0:T(4,128)S(1)} %maximum_select_fusion.1), channel_id=1, source_target_pairs={{0,64},{16,80},{32,96},{48,112},{64,128},{80,144},{96,160},{112,17... | collective-permute-start | bytes 792584 | tf_op jit(solution)/shard_map/ppermute | solution.py:95
  52.7 20.8 %collective-permute-start.5 = (f32[4,16512]{1,0:T(4,128)S(1)}, f32[4,16512]{1,0:T(4,128)S(1)}, u32[]{:S(2)}, u32[]{:S(2)}) collective-permute-start(f32[4,16512]{1,0:T(4,128)S(1)} %maximum_select_fusion.2), channel_id=1, source_target_pairs={{0,128},{16,144},{32,160},{48,176},{64,192},{80,208},{96,224},{112... | collective-permute-start | bytes 792584 | tf_op jit(solution)/shard_map/ppermute | solution.py:95
  61.9 12.4 %copy-start.1 = (bf16[128,1024]{1,0:T(8,128)(2,1)S(1)}, bf16[128,1024]{1,0:T(8,128)(2,1)}, u32[]{:S(2)}) copy-start(bf16[128,1024]{1,0:T(8,128)(2,1)} %param.8) | copy-start | bytes 786436
  61.9 14.5 %copy-start.2 = (bf16[128,1024]{1,0:T(8,128)(2,1)S(1)}, bf16[128,1024]{1,0:T(8,128)(2,1)}, u32[]{:S(2)}) copy-start(bf16[128,1024]{1,0:T(8,128)(2,1)} %param.10) | copy-start | bytes 786436
  61.9 156.0 %copy-start.4 = (bf16[128,1024]{1,0:T(8,128)(2,1)S(1)}, bf16[128,1024]{1,0:T(8,128)(2,1)}, u32[]{:S(2)}) copy-start(bf16[128,1024]{1,0:T(8,128)(2,1)} %param.11) | copy-start | bytes 786436
  61.9 156.0 %copy-start.5 = (f32[1024]{0:T(1024)S(1)}, f32[1024]{0:T(1024)}, u32[]{:S(2)}) copy-start(f32[1024]{0:T(1024)} %param.14) | copy-start | bytes 12292
  61.9 156.0 %all-to-all-start = ((bf16[32,1024,192]{1,2,0:T(8,128)(2,1)}), bf16[32,1024,192]{1,2,0:T(8,128)(2,1)}, u32[]{:S(2)}, u32[]{:S(2)}) async-start(bf16[32,1024,192]{1,2,0:T(8,128)(2,1)} %stack.2), calls=%async_computation | async-start | bytes 25165824 | tf_op jit(solution)/shard_map/all_to_all | solution.py:138
  73.2 216.1 %reduce-scatter.2.cloned.1.call-start = ((), (), s32[]{:S(2)}) async-start(), calls=%async_computation.2 | async-start | bytes 3538944 | tf_op jit(solution)/shard_map/reduce_scatter | solution.py:145
  74.0 1.6 collective-permute-start.6
Sparse Core Ops, SparseCore 0:
  228.5 60.6 reduce-scatter.1
